TPU v7x, 32 devices: a whole 2x2x4 slice. The times are simulated.
32 devices in a mesh: dp: 8 (over z, x), tensor: 4 (over y, core).
Axes of the slice: x: 2, y: 2, z: 4, core: 2. Of those that a mesh axis runs over, the one named last changes fastest.
Arguments:
- images_in: bfloat16 [32, 544, 768], P(('dp', 'tensor')), may hold values from -6 to 6
- crop_lengths: int32 [32, 6], P('dp'), may hold values from 1 to 197, 544 in all within a row
- route_index: int32 [32, 272], P('dp'), may hold values from 0 to 543, as said below
- router_weight: bfloat16 [768], replicated, may hold values from -0.21875 to 0.21875
- norm_gain: bfloat16 [2, 2, 768], replicated, may hold values from 0.5 to 1.5
- norm_shift: bfloat16 [2, 2, 768], replicated, may hold values from -1.75 to 1.75
- qkv_weight: bfloat16 [2, 3, 768, 768], P(None, None, None, 'tensor'), may hold values from -0.21875 to 0.21875
- qv_bias: bfloat16 [2, 2, 768], P(None, None, 'tensor'), may hold values from -3 to 3
- out_weight: bfloat16 [2, 768, 768], P(None, 'tensor'), may hold values from -0.75 to 0.75
- out_bias: bfloat16 [2, 768], replicated, may hold values from -1.75 to 1.75
- fc1_weight: bfloat16 [2, 768, 3072], P(None, None, 'tensor'), may hold values from -0.21875 to 0.21875
- fc1_bias: bfloat16 [2, 3072], P(None, 'tensor'), may hold values from -3 to 3
- fc2_weight: bfloat16 [2, 3072, 768], P(None, 'tensor'), may hold values from -0.109375 to 0.109375
- fc2_bias: bfloat16 [2, 768], replicated, may hold values from -1.75 to 1.75
- out_cotangent: bfloat16 [32, 544, 768], P(('dp', 'tensor')), may hold values from -6 to 6
Outputs:
- images_out: bfloat16 [32, 544, 768], P(('dp', 'tensor'))
- input_grad: float32 [32, 544, 768], P(('dp', 'tensor'))
- router_grad: float32 [768], replicated
- gain_grad: float32 [2, 2, 768], replicated
- shift_grad: float32 [2, 2, 768], replicated
- qkv_grad: float32 [2, 3, 768, 768], P(None, None, None, 'tensor')
- qv_bias_grad: float32 [2, 2, 768], P(None, None, 'tensor')
- out_weight_grad: float32 [2, 768, 768], P(None, 'tensor')
- out_bias_grad: float32 [2, 768], replicated
- fc1_grad: float32 [2, 768, 3072], P(None, None, 'tensor')
- fc1_bias_grad: float32 [2, 3072], P(None, 'tensor')
- fc2_grad: float32 [2, 3072, 768], P(None, 'tensor')
- fc2_bias_grad: float32 [2, 768], replicated
Inputs may be any that keep to these rules, and one draw needn't show every extreme that they name: `route_index`: within each image the 272 positions are distinct and ascending.
All inputs are finite; a program needn't handle non-finite values.
Results may differ from a plain program's by a relative error of at most 0.02.
Values may be sent and summed in bfloat16 or wider, within the bound.
A program may use at most 256 MiB of HBM per device.

v0:
```python
import jax
import jax.numpy as jnp
from jax import lax
from jax.sharding import PartitionSpec as P

HEAD_DIM = 64
norm_eps = 1e-06
mask_fill = -1e30
half_root = 0.7071067811865476
inv_root_tau = 0.3989422804014327


def crop_index(lengths, positions):
    bounds = jnp.cumsum(lengths, axis=-1)
    above = positions[:, :, None] >= bounds[:, None, :]
    return jnp.sum(above.astype(jnp.int32), axis=-1)


def norm_rows(inputs, gain_row, shift_row):
    row_mean = jnp.mean(inputs, axis=-1, keepdims=True)
    centred = inputs - row_mean
    inv_std = lax.rsqrt(jnp.mean(centred * centred, axis=-1, keepdims=True) + norm_eps)
    normalised = centred * inv_std
    return (normalised, inv_std, (normalised * gain_row + shift_row).astype(jnp.bfloat16))


def norm_back(gradient, normalised, inv_std, gain_row):
    features = gradient.shape[-1]
    scaled = gradient * gain_row
    inner = jnp.mean(scaled, axis=-1, keepdims=True) + normalised * jnp.mean(
        scaled * normalised, axis=-1, keepdims=True
    )
    gain_part = jnp.sum((gradient * normalised).reshape(-1, features), axis=0)
    shift_part = jnp.sum(gradient.reshape(-1, features), axis=0)
    return (inv_std * (scaled - inner), gain_part, shift_part)


def gelu_value(preact):
    return 0.5 * preact * (1.0 + lax.erf(preact * half_root))


def gelu_slope(preact):
    return 0.5 * (1.0 + lax.erf(preact * half_root)) + preact * inv_root_tau * jnp.exp(
        -0.5 * preact * preact
    )


def block_images(images_all, length):
    per_block = 1
    while per_block * length < 512 and images_all % (2 * per_block) == 0:
        per_block = per_block * 2
    return per_block


def by_blocks(function, arrays, per_block):
    shaped = jax.tree.map(
        lambda item: item.reshape((item.shape[0] // per_block, per_block) + item.shape[1:]), arrays
    )
    result = lax.map(function, shaped)
    return jax.tree.map(
        lambda item: item.reshape((item.shape[0] * item.shape[1],) + item.shape[2:]), result
    )


def masked_scores(queries, key_rows, crops):
    scale = queries.shape[-1] ** (-0.5)
    raw_scores = (
        jnp.einsum("gqhe,gkhe->ghqk", queries, key_rows, preferred_element_type=jnp.float32) * scale
    )
    same_crop = (crops[:, :, None] == crops[:, None, :])[:, None]
    return jnp.where(same_crop, raw_scores, mask_fill)


def attend_block(block_parts):
    queries, key_rows, values, crops = block_parts
    scores = masked_scores(queries, key_rows, crops)
    row_max = jnp.max(scores, axis=-1, keepdims=True)
    exponent = jnp.exp(scores - row_max)
    row_total = jnp.sum(exponent, axis=-1, keepdims=True)
    attn_probs = (exponent / row_total).astype(jnp.bfloat16)
    head_out = jnp.einsum("ghqk,gkhe->gqhe", attn_probs, values, preferred_element_type=jnp.float32)
    return (head_out.astype(jnp.bfloat16), (row_max + jnp.log(row_total))[..., 0])


def attend_back(block_parts):
    queries, key_rows, values, head_grads, log_total, crops = block_parts
    scale = queries.shape[-1] ** (-0.5)
    scores = masked_scores(queries, key_rows, crops)
    attn_probs = jnp.exp(scores - log_total[..., None])
    low_probs = attn_probs.astype(jnp.bfloat16)
    value_grad = jnp.einsum(
        "ghqk,gqhe->gkhe", low_probs, head_grads, preferred_element_type=jnp.float32
    )
    prob_grad = jnp.einsum(
        "gqhe,gkhe->ghqk", head_grads, values, preferred_element_type=jnp.float32
    )
    score_grad = (
        attn_probs * (prob_grad - jnp.sum(attn_probs * prob_grad, axis=-1, keepdims=True))
    ).astype(jnp.bfloat16)
    query_grad = (
        jnp.einsum("ghqk,gkhe->gqhe", score_grad, key_rows, preferred_element_type=jnp.float32)
        * scale
    )
    key_grad = (
        jnp.einsum("ghqk,gqhe->gkhe", score_grad, queries, preferred_element_type=jnp.float32)
        * scale
    )
    return (
        query_grad.astype(jnp.bfloat16),
        key_grad.astype(jnp.bfloat16),
        value_grad.astype(jnp.bfloat16),
    )


def attention_forward(
    inputs, crops_all, gain_row, shift_row, qkv_weights, qv_biases, out_weights, out_biases
):
    normalised, inv_std, normed = norm_rows(inputs, gain_row, shift_row)
    gathered = lax.all_gather(normed, "tensor", axis=0, tiled=True)
    images_all, length, features = gathered.shape
    local_width = qkv_weights.shape[-1]
    head_shape = (images_all, length, local_width // HEAD_DIM, HEAD_DIM)
    projected = jnp.einsum(
        "gld,cde->glce", gathered, qkv_weights, preferred_element_type=jnp.float32
    )
    queries = (projected[:, :, 0] + qv_biases[0]).astype(jnp.bfloat16).reshape(head_shape)
    key_rows = projected[:, :, 1].astype(jnp.bfloat16).reshape(head_shape)
    values = (projected[:, :, 2] + qv_biases[1]).astype(jnp.bfloat16).reshape(head_shape)
    per_block = block_images(images_all, length)
    head_out, log_total = by_blocks(attend_block, (queries, key_rows, values, crops_all), per_block)
    head_out = head_out.reshape(images_all, length, local_width)
    branch = (
        lax.psum_scatter(
            jnp.einsum("gle,ed->gld", head_out, out_weights, preferred_element_type=jnp.float32),
            "tensor",
            scatter_dimension=0,
            tiled=True,
        )
        + out_biases
    )
    out_keep = (head_out, out_weights)
    kept = (normalised, inv_std, gathered, queries, key_rows, values, log_total, out_keep)
    return (branch, kept)


def attention_back(gradient, kept, crops_all, gain_row, qkv_weights):
    normalised, inv_std, gathered, queries, key_rows, values, log_total, out_keep = kept
    own_count, length, features = gradient.shape
    grad_low = gradient.astype(jnp.bfloat16)
    out_bias_part = jnp.sum(grad_low.reshape(-1, features), axis=0, dtype=jnp.float32)
    images_all = queries.shape[0]
    local_width = queries.shape[2] * queries.shape[3]
    head_out, out_weights = out_keep
    grad_all = lax.all_gather(grad_low, "tensor", axis=0, tiled=True)
    out_part = jnp.einsum("gle,gld->ed", head_out, grad_all, preferred_element_type=jnp.float32)
    head_grads = jnp.einsum(
        "gld,ed->gle", grad_all, out_weights, preferred_element_type=jnp.float32
    )
    head_grads = head_grads.astype(jnp.bfloat16).reshape(queries.shape)
    per_block = block_images(images_all, length)
    query_grad, key_grad, value_grad = by_blocks(
        attend_back, (queries, key_rows, values, head_grads, log_total, crops_all), per_block
    )
    qv_part = jnp.stack(
        [
            jnp.sum(query_grad.reshape(-1, local_width), axis=0, dtype=jnp.float32),
            jnp.sum(value_grad.reshape(-1, local_width), axis=0, dtype=jnp.float32),
        ]
    )
    proj_grad = jnp.stack([query_grad, key_grad, value_grad], axis=2).reshape(
        images_all, length, 3, local_width
    )
    qkv_part = jnp.einsum("gld,glce->cde", gathered, proj_grad, preferred_element_type=jnp.float32)
    normed_grad = lax.psum_scatter(
        jnp.einsum(
            "glce,cde->gld", proj_grad, qkv_weights, preferred_element_type=jnp.float32
        ).astype(jnp.bfloat16),
        "tensor",
        scatter_dimension=0,
        tiled=True,
    ).astype(jnp.float32)
    input_part, gain_part, shift_part = norm_back(normed_grad, normalised, inv_std, gain_row)
    return (input_part, (gain_part, shift_part, qkv_part, qv_part, out_part, out_bias_part))


def dense_forward(
    inputs, gain_row, shift_row, first_weights, first_biases, second_weights, second_biases
):
    normalised, inv_std, normed = norm_rows(inputs, gain_row, shift_row)
    full_first, full_first_bias, full_second = (
        lax.all_gather(first_weights, "tensor", axis=1, tiled=True),
        lax.all_gather(first_biases, "tensor", axis=0, tiled=True),
        lax.all_gather(second_weights, "tensor", axis=0, tiled=True),
    )
    preact = (
        jnp.einsum("gld,df->glf", normed, full_first, preferred_element_type=jnp.float32)
        + full_first_bias
    )
    hidden = gelu_value(preact).astype(jnp.bfloat16)
    branch = (
        jnp.einsum("glf,fd->gld", hidden, full_second, preferred_element_type=jnp.float32)
        + second_biases
    )
    kept = (normalised, inv_std, normed, preact, hidden, full_first, full_second)
    return (branch, kept)


def dense_back(gradient, kept, gain_row):
    normalised, inv_std, normed, preact, hidden, first_weights, second_weights = kept
    own_count, length, features = gradient.shape
    grad_low = gradient.astype(jnp.bfloat16)
    second_bias_part = jnp.sum(grad_low.reshape(-1, features), axis=0, dtype=jnp.float32)
    second_part = jnp.einsum("glf,gld->fd", hidden, grad_low, preferred_element_type=jnp.float32)
    hidden_grad = jnp.einsum(
        "gld,fd->glf", grad_low, second_weights, preferred_element_type=jnp.float32
    )
    pre_grad = (hidden_grad * gelu_slope(preact)).astype(jnp.bfloat16)
    first_bias_part = jnp.sum(pre_grad.reshape(-1, pre_grad.shape[-1]), axis=0, dtype=jnp.float32)
    first_part = jnp.einsum("gld,glf->df", normed, pre_grad, preferred_element_type=jnp.float32)
    normed_grad = jnp.einsum(
        "glf,df->gld", pre_grad, first_weights, preferred_element_type=jnp.float32
    )
    first_part, first_bias_part, second_part = (
        lax.psum_scatter(
            first_part.astype(jnp.bfloat16), "tensor", scatter_dimension=1, tiled=True
        ).astype(jnp.float32),
        lax.psum_scatter(
            first_bias_part.astype(jnp.bfloat16), "tensor", scatter_dimension=0, tiled=True
        ).astype(jnp.float32),
        lax.psum_scatter(
            second_part.astype(jnp.bfloat16), "tensor", scatter_dimension=0, tiled=True
        ).astype(jnp.float32),
    )
    input_part, gain_part, shift_part = norm_back(normed_grad, normalised, inv_std, gain_row)
    return (
        input_part,
        (gain_part, shift_part, first_part, first_bias_part, second_part, second_bias_part),
    )


def body(
    images_in,
    crop_lengths,
    route_index,
    router_weight,
    norm_gain,
    norm_shift,
    qkv_weight,
    qv_bias,
    out_weight,
    out_bias,
    fc1_weight,
    fc1_bias,
    fc2_weight,
    fc2_bias,
    out_cotangent,
):
    own_count, length, features = images_in.shape
    images_all = crop_lengths.shape[0]
    offset = lax.axis_index("tensor") * own_count
    positions = jnp.broadcast_to(jnp.arange(length, dtype=jnp.int32), (images_all, length))
    crops_full = crop_index(crop_lengths, positions)
    crops_chosen = jnp.take_along_axis(crops_full, route_index, axis=1)
    own_index = lax.dynamic_slice_in_dim(route_index, offset, own_count, 0)
    row_index = jnp.arange(own_count, dtype=jnp.int32)[:, None]
    chosen = images_in[row_index, own_index]
    chosen_data = chosen.astype(jnp.float32)
    router_data = router_weight.astype(jnp.float32)
    router_logit = jnp.einsum(
        "nsd,d->ns", chosen, router_weight, preferred_element_type=jnp.float32
    )
    route_rate = 1.0 / (1.0 + jnp.exp(-router_logit))
    attn_one, kept_one = attention_forward(
        chosen_data,
        crops_chosen,
        norm_gain[0, 0],
        norm_shift[0, 0],
        qkv_weight[0],
        qv_bias[0],
        out_weight[0],
        out_bias[0],
    )
    middle = chosen_data + attn_one
    ffn_one, kept_two = dense_forward(
        middle,
        norm_gain[0, 1],
        norm_shift[0, 1],
        fc1_weight[0],
        fc1_bias[0],
        fc2_weight[0],
        fc2_bias[0],
    )
    branches = attn_one + ffn_one
    routed = (
        images_in.astype(jnp.float32)
        .at[row_index, own_index]
        .add(route_rate[:, :, None] * branches)
    )
    attn_two, kept_three = attention_forward(
        routed,
        crops_full,
        norm_gain[1, 0],
        norm_shift[1, 0],
        qkv_weight[1],
        qv_bias[1],
        out_weight[1],
        out_bias[1],
    )
    after_attn = routed + attn_two
    ffn_two, kept_four = dense_forward(
        after_attn,
        norm_gain[1, 1],
        norm_shift[1, 1],
        fc1_weight[1],
        fc1_bias[1],
        fc2_weight[1],
        fc2_bias[1],
    )
    images_out = (after_attn + ffn_two).astype(jnp.bfloat16)
    cotangent = out_cotangent.astype(jnp.float32)
    back_four, grads_four = dense_back(cotangent, kept_four, norm_gain[1, 1])
    grad_after = cotangent + back_four
    back_three, grads_three = attention_back(
        grad_after, kept_three, crops_full, norm_gain[1, 0], qkv_weight[1]
    )
    grad_routed = grad_after + back_three
    grad_chosen = grad_routed[row_index, own_index]
    logit_grad = jnp.sum(grad_chosen * branches, axis=-1) * route_rate * (1.0 - route_rate)
    router_part = jnp.einsum("nsd,ns->d", chosen_data, logit_grad, precision=lax.Precision.HIGHEST)
    branch_grad = route_rate[:, :, None] * grad_chosen
    back_two, grads_two = dense_back(branch_grad, kept_two, norm_gain[0, 1])
    back_one, grads_one = attention_back(
        branch_grad + back_two, kept_one, crops_chosen, norm_gain[0, 0], qkv_weight[0]
    )
    own_grad = logit_grad[:, :, None] * router_data + back_two + back_one
    input_grad = grad_routed.at[row_index, own_index].add(own_grad)
    gain_part = jnp.stack(
        [jnp.stack([grads_one[0], grads_two[0]]), jnp.stack([grads_three[0], grads_four[0]])]
    )
    shift_part = jnp.stack(
        [jnp.stack([grads_one[1], grads_two[1]]), jnp.stack([grads_three[1], grads_four[1]])]
    )
    out_bias_part = jnp.stack([grads_one[5], grads_three[5]])
    second_bias_part = jnp.stack([grads_two[5], grads_four[5]])
    shared = lax.psum(
        (router_part, gain_part, shift_part, out_bias_part, second_bias_part), ("dp", "tensor")
    )
    qkv_part = jnp.stack([grads_one[2], grads_three[2]])
    qv_part = jnp.stack([grads_one[3], grads_three[3]])
    out_part = jnp.stack([grads_one[4], grads_three[4]])
    first_part = jnp.stack([grads_two[2], grads_four[2]])
    first_bias_part = jnp.stack([grads_two[3], grads_four[3]])
    second_part = jnp.stack([grads_two[4], grads_four[4]])
    split = (
        lax.psum(qkv_part.astype(jnp.bfloat16), "dp").astype(jnp.float32),
        lax.psum(qv_part.astype(jnp.bfloat16), "dp").astype(jnp.float32),
        lax.psum(out_part.astype(jnp.bfloat16), "dp").astype(jnp.float32),
        lax.psum(first_part.astype(jnp.bfloat16), "dp").astype(jnp.float32),
        lax.psum(first_bias_part.astype(jnp.bfloat16), "dp").astype(jnp.float32),
        lax.psum(second_part.astype(jnp.bfloat16), "dp").astype(jnp.float32),
    )
    return (
        images_out,
        input_grad,
        shared[0],
        shared[1],
        shared[2],
        split[0],
        split[1],
        split[2],
        shared[3],
        split[3],
        split[4],
        split[5],
        shared[4],
    )


def solution(mesh):
    in_specs = (
        P(("dp", "tensor"), None, None),
        P("dp", None),
        P("dp", None),
        P(),
        P(),
        P(),
        P(None, None, None, "tensor"),
        P(None, None, "tensor"),
        P(None, "tensor", None),
        P(),
        P(None, None, "tensor"),
        P(None, "tensor"),
        P(None, "tensor", None),
        P(),
        P(("dp", "tensor"), None, None),
    )
    out_specs = (
        P(("dp", "tensor"), None, None),
        P(("dp", "tensor"), None, None),
        P(),
        P(),
        P(),
        P(None, None, None, "tensor"),
        P(None, None, "tensor"),
        P(None, "tensor", None),
        P(),
        P(None, None, "tensor"),
        P(None, "tensor"),
        P(None, "tensor", None),
        P(),
    )
    return jax.shard_map(body, mesh=mesh, in_specs=in_specs, out_specs=out_specs, check_vma=False)
```

profile of v0, /device:TPU:0, one launch (start us, length us, event | category | flops | bytes accessed | tf_op | source)
XLA Modules:
  0.0 1083.5 jit_solution(4589102543825514392)
XLA Ops:
  8.0 13.7 %gather_fusion = bf16[272,768]{1,0:T(8,128)(2,1)S(1)} fusion(bf16[1,544,768]{2,1,0:T(8,128)(2,1)} %param.23, s32[272]{0:T(512)S(1)} %get-tuple-element.320), kind=kCustom, calls=%fused_computation | custom fusion | bytes 837760 | tf_op jit(solution)/shard_map/gather | solution.py:266
  24.1 9.3 gather_fusion.2
  33.6 12.8 %all-gather.15.cloned.1.call-done = bf16[4,272,768]{2,1,0:T(8,128)(2,1)} async-done(((bf16[1,272,768]{2,1,0:T(8,128)(2,1)}), bf16[4,272,768]{2,1,0:T(8,128)(2,1)}) %all-gather.15.cloned.1.call-update) | async-done | bytes 1671184 | tf_op jit(solution)/shard_map/all_gather | solution.py:119
  46.5 2.9 fusion.158
  55.6 5.0 while.52
  63.3 3.2 fusion.273
  66.6 3.2 fusion.272
  69.9 5.6 all-gather.1
  76.7 25.8 %reduce-scatter.9.cloned.1.call-done = f32[1,272,768]{2,1,0:T(8,128)} async-done(((f32[4,272,768]{2,1,0:T(8,128)}), f32[1,272,768]{2,1,0:T(8,128)}) %reduce-scatter.9.cloned.1.call-update) | async-done | bytes 835600 | tf_op jit(solution)/shard_map/reduce_scatter | solution.py:133
  104.1 38.0 %all-gather.23.cloned.1.call-done = bf16[1,768,3072]{2,1,0:T(8,128)(2,1)} async-done(((bf16[1,768,768]{2,1,0:T(8,128)(2,1)}), bf16[1,768,3072]{2,1,0:T(8,128)(2,1)}) %all-gather.23.cloned.1.call-update) | async-done | bytes 4718608 | tf_op jit(solution)/shard_map/all_gather | solution.py:191
  142.2 6.1 multiply_convert_fusion.3
  148.3 33.4 %all-gather.25.cloned.1.call-done = bf16[1,3072,768]{2,1,0:T(8,128)(2,1)} async-done(((bf16[1,768,768]{2,1,0:T(8,128)(2,1)}), bf16[1,3072,768]{2,1,0:T(8,128)(2,1)}) %all-gather.25.cloned.1.call-update) | async-done | bytes 4718608 | tf_op jit(solution)/shard_map/all_gather | solution.py:193
  181.7 4.5 fusion.184
  186.3 3.1 scatter_custom_fusion
  191.6 29.4 %all-gather.17.cloned.1.call-done = bf16[4,544,768]{2,1,0:T(8,128)(2,1)} async-done(((bf16[1,544,768]{2,1,0:T(8,128)(2,1)}), bf16[4,544,768]{2,1,0:T(8,128)(2,1)}) %all-gather.17.cloned.1.call-update) | async-done | bytes 3342352 | tf_op jit(solution)/shard_map/all_gather | solution.py:119
  221.0 4.7 fusion.147
  229.4 25.0 %while.53 = (s32[]{:T(128)}, bf16[4,1,544,3,64]{2,4,3,1,0:T(8,128)(2,1)}, f32[4,1,3,544]{3,2,1,0:T(4,128)S(1)}, bf16[4,1,544,3,64]{2,4,3,1,0:T(8,128)(2,1)}, s32...) while((s32[]{:T(128)}, ...), condition=%wide.region_17.18_spmd, body=%wide.region_14.17_spmd.sunk | while | flops 238331296 | bytes 12944741 | solution.py:59
  232.6 3.0 fusion.342
  238.8 3.0 fusion.342
  245.1 3.0 fusion.342
  251.3 3.0 fusion.342
  254.4 5.1 fusion.243
  261.1 5.4 all-gather.4
  266.4 54.2 %reduce-scatter.11.cloned.1.call-done = f32[1,544,768]{2,1,0:T(8,128)} async-done(((f32[4,544,768]{2,1,0:T(8,128)}), f32[1,544,768]{2,1,0:T(8,128)}) %reduce-scatter.11.cloned.1.call-update) | async-done | bytes 1671184 | tf_op jit(solution)/shard_map/reduce_scatter | solution.py:133
  323.9 36.4 %all-gather.27.cloned.1.call-done = bf16[1,768,3072]{2,1,0:T(8,128)(2,1)} async-done(((bf16[1,768,768]{2,1,0:T(8,128)(2,1)}), bf16[1,768,3072]{2,1,0:T(8,128)(2,1)}) %all-gather.27.cloned.1.call-update) | async-done | bytes 4718608 | tf_op jit(solution)/shard_map/all_gather | solution.py:191
  360.3 8.7 multiply_convert_fusion.2
  368.9 31.0 %all-gather.29.cloned.1.call-done = bf16[1,3072,768]{2,1,0:T(8,128)(2,1)} async-done(((bf16[1,768,768]{2,1,0:T(8,128)(2,1)}), bf16[1,3072,768]{2,1,0:T(8,128)(2,1)}) %all-gather.29.cloned.1.call-update) | async-done | bytes 4718608 | tf_op jit(solution)/shard_map/all_gather | solution.py:193
  399.9 8.4 fusion.275
  408.4 3.6 fusion.160
  412.7 2.7 convert_reduce_fusion.2
  415.9 29.4 %all-gather.19.cloned.1.call-done = bf16[4,544,768]{2,1,0:T(8,128)(2,1)} async-done(((bf16[1,544,768]{2,1,0:T(8,128)(2,1)}), bf16[4,544,768]{2,1,0:T(8,128)(2,1)}) %all-gather.19.cloned.1.call-update) | async-done | bytes 3342352 | tf_op jit(solution)/shard_map/all_gather | solution.py:154
  445.3 4.1 convolution_convert_fusion.4
  452.7 45.8 %while.54 = (s32[]{:T(128)}, bf16[4,1,544,3,64]{2,4,3,1,0:T(8,128)(2,1)}, bf16[4,1,544,3,64]{2,4,3,1,0:T(8,128)(2,1)}, bf16[4,1,544,3,64]{2,4,3,1,0:T(8,128)(2,1...) while((s32[]{:T(128)}, ...), condition=%wide.region_25.26_spmd, body=%wide.region_23.25_spmd.sunk | while | flops 582330752 | bytes 35354008 | solution.py:59
  454.8 2.5 multiply_reduce_fusion.9
  466.3 2.5 multiply_reduce_fusion.9
  477.8 2.5 multiply_reduce_fusion.9
  489.2 2.5 multiply_reduce_fusion.9
  498.5 6.6 bitcast_convert_fusion
  505.4 39.1 %reduce-scatter.13.cloned.1.call-done = bf16[1,544,768]{2,1,0:T(8,128)(2,1)} async-done(((bf16[4,544,768]{2,1,0:T(8,128)(2,1)}), bf16[1,544,768]{2,1,0:T(8,128)(2,1)}) %reduce-scatter.13.cloned.1.call-update) | async-done | bytes 835600 | tf_op jit(solution)/shard_map/reduce_scatter | solution.py:174
  548.6 4.3 gather_fusion.1
  553.9 7.1 fusion.276
  561.0 5.2 fusion.216
  568.8 7.7 convolution_convert_fusion.3
  577.7 6.0 convolution_convert_fusion.1
  584.9 7.6 convolution_convert_fusion.2
  593.5 6.2 convolution_convert_fusion
  600.9 3.2 convolution_convert_fusion.5
  608.3 13.0 %while.55 = (s32[]{:T(128)}, bf16[2,2,272,3,64]{2,4,3,1,0:T(8,128)(2,1)}, bf16[2,2,272,3,64]{2,4,3,1,0:T(8,128)(2,1)}, bf16[2,2,272,3,64]{2,4,3,1,0:T(8,128)(2,1...) while((s32[]{:T(128)}, ...), condition=%wide.region_34.35_spmd, body=%wide.region_32.34_spmd.sunk | while | flops 288762272 | bytes 28893860 | solution.py:59
  625.3 4.1 bitcast_convert_fusion.1
  629.8 3.3 fusion.190
  641.2 49.9 %reduce-scatter.17.cloned.1.call-done = bf16[768,768]{1,0:T(8,128)(2,1)} async-done(((bf16[768,3072]{1,0:T(8,128)(2,1)}), bf16[768,768]{1,0:T(8,128)(2,1)}) %reduce-scatter.17.cloned.1.call-update) | async-done | bytes 1179664 | tf_op jit(solution)/shard_map/reduce_scatter | solution.py:224
  691.2 3.2 pad_maximum_fusion.1
  694.4 47.2 %reduce-scatter.23.cloned.1.call-done = bf16[768,768]{1,0:T(8,128)(2,1)} async-done(((bf16[3072,768]{1,0:T(8,128)(2,1)}), bf16[768,768]{1,0:T(8,128)(2,1)}) %reduce-scatter.23.cloned.1.call-update) | async-done | bytes 1179664 | tf_op jit(solution)/shard_map/reduce_scatter | solution.py:230
  741.6 50.3 %reduce-scatter.21.cloned.1.call-done = bf16[768,768]{1,0:T(8,128)(2,1)} async-done(((bf16[3072,768]{1,0:T(8,128)(2,1)}), bf16[768,768]{1,0:T(8,128)(2,1)}) %reduce-scatter.21.cloned.1.call-update) | async-done | bytes 1179664 | tf_op jit(solution)/shard_map/reduce_scatter | solution.py:230
  791.9 3.2 pad_maximum_fusion.2
  800.1 8.0 fusion.164
  821.5 11.3 %all-reduce.6 = (bf16[3072]{0:T(1024)(128)(2,1)}, bf16[3072]{0:T(1024)(128)(2,1)}) all-reduce(bf16[3072]{0:T(1024)(128)(2,1)} %get-tuple-element.443, bf16[3072]{0:T(1024)(128)(2,1)} %get-tuple-element.445), channel_id=15, replica_groups=mesh['dp'=8,'tensor'=4] {'tensor'}, use_global_device_ids=true, to_apply=%region_66.67.clone | all-reduce | flops 6144 | bytes 24576
  846.5 23.4 %all-reduce.4 = (bf16[2,2,192]{2,1,0:T(2,128)(2,1)S(1)}, bf16[2,768]{1,0:T(2,128)(2,1)S(1)}) all-reduce(bf16[2,2,192]{2,1,0:T(2,128)(2,1)S(1)} %pad_maximum_fusion.15, bf16[2,768]{1,0:T(2,128)(2,1)} %pad_maximum_fusion.14), channel_id=1, replica_groups=mesh['dp'=8,'tensor'=4] {'dp'}, use_global_device_ids=true, to_apply=%region_55.56 | all-reduce | flops 2304 | bytes 9216 | tf_op jit(solution)/shard_map/psum | solution.py:356
  872.7 4.3 scatter_custom_fusion.1
  877.2 41.6 %all-reduce.3 = (f32[768]{0:T(1024)}, f32[2,2,768]{2,1,0:T(2,128)}, f32[2,2,768]{2,1,0:T(2,128)}, f32[2,768]{1,0:T(2,128)}, f32[2,768]{1,0:T(2,128)}) all-reduce(f32[768]{0:T(1024)S(1)} %copy-done.82, f32[2,2,768]{2,1,0:T(2,128)S(1)} %pad_maximum_fusion.10, ...), channel_id=1, replica_groups=mesh['dp'=8,'tensor'=4] {'dp','tensor'}, use_global_device_ids=true, to_apply=%region_39.40 | all-reduce | flops 9984 | bytes 79872 | tf_op jit(solution)/shard_map/psum | solution.py:345
  918.8 147.8 %all-reduce.9.cloned.1.call-done = (bf16[2,3,768,192]{2,3,1,0:T(8,128)(2,1)}, bf16[2,192,768]{2,1,0:T(8,128)(2,1)}, bf16[2,768,768]{2,1,0:T(8,128)(2,1)}, bf16[2,768,768]{2,1,0:T(8,128)(2,1)}) async-done(((bf16[2,3,768,192]{2,3,1,0:T(8,128)(2,1)}, bf16[2,192,768]{2,1,0:T(8,128)(2,1)}, bf16[2,768,768]{2,1,0:T(8,128)(2,1)}, bf16[2,768,768]{2,1,0:T(8,128)(2,1)}), (bf16[2,3,768,192]{2,3,1,0:T(8,128)(2,1)}, ...) | async-done | bytes 7077904 | tf_op jit(solution)/shard_map/psum | solution.py:355
  1066.6 3.7 convert_element_type.429
  1071.4 2.5 convert_element_type.440
  1074.0 2.5 convert_element_type.444
  (487 shorter events, 159.9 us)
Async XLA Ops:
  7.2 15.1 %copy-start.71 = (bf16[2,2,768]{2,1,0:T(2,128)(2,1)S(1)}, bf16[2,2,768]{2,1,0:T(2,128)(2,1)}, u32[]{:S(2)}) copy-start(bf16[2,2,768]{2,1,0:T(2,128)(2,1)} %param.28) | copy-start | bytes 18436
  7.2 15.1 %copy-start.72 = (bf16[2,2,768]{2,1,0:T(2,128)(2,1)S(1)}, bf16[2,2,768]{2,1,0:T(2,128)(2,1)}, u32[]{:S(2)}) copy-start(bf16[2,2,768]{2,1,0:T(2,128)(2,1)} %param.27) | copy-start | bytes 18436
  7.2 39.3 %all-gather.15.cloned.1.call-start = ((), (), s32[]{:S(2)}) async-start(), calls=%async_computation.8 | async-start | bytes 2088960 | tf_op jit(solution)/shard_map/all_gather | solution.py:119
  8.0 15.4 %copy-start.5 = (s32[272]{0:T(512)}, s32[272]{0:T(512)S(1)}, u32[]{:S(2)}) copy-start(s32[272]{0:T(512)S(1)} %get-tuple-element.320) | copy-start | bytes 3268
  8.0 178.3 %copy-start.97 = (s32[272]{0:T(512)}, s32[272]{0:T(512)S(1)}, u32[]{:S(2)}) copy-start(s32[272]{0:T(512)S(1)} %get-tuple-element.321) | copy-start | bytes 3268
  8.0 15.5 %copy-start.92 = (bf16[2,2,192]{2,1,0:T(2,128)(2,1)S(1)}, bf16[2,2,192]{2,1,0:T(2,128)(2,1)}, u32[]{:S(2)}) copy-start(bf16[2,2,192]{2,1,0:T(2,128)(2,1)} %param.30) | copy-start | bytes 4612
  8.0 15.6 %copy-start.98 = (s32[4,6]{1,0:T(4,128)S(1)}, s32[4,6]{1,0:T(4,128)}, u32[]{:S(2)}) copy-start(s32[4,6]{1,0:T(4,128)} %param.24) | copy-start | bytes 292
  8.0 15.8 %copy-start.70 = (s32[4,272]{1,0:T(4,128)S(1)}, s32[4,272]{1,0:T(4,128)}, u32[]{:S(2)}) copy-start(s32[4,272]{1,0:T(4,128)} %param.25) | copy-start | bytes 13060
  21.8 80.7 %copy-start.7 = (bf16[272,768]{1,0:T(8,128)(2,1)}, bf16[272,768]{1,0:T(8,128)(2,1)S(1)}, u32[]{:S(2)}) copy-start(bf16[272,768]{1,0:T(8,128)(2,1)S(1)} %gather_fusion) | copy-start | bytes 1253380
  22.3 119.8 %copy-start.60 = (f32[768]{0:T(1024)}, f32[768]{0:T(1024)S(1)}, u32[]{:S(2)}) copy-start(f32[768]{0:T(1024)S(1)} %get-tuple-element.449) | copy-start | bytes 9220
  22.4 119.8 %copy-start.93 = (f32[768]{0:T(1024)}, f32[768]{0:T(1024)S(1)}, u32[]{:S(2)}) copy-start(f32[768]{0:T(1024)S(1)} %get-tuple-element.313) | copy-start | bytes 9220
  23.4 79.0 %reduce-scatter.9.cloned.1.call-start = ((), (), s32[]{:S(2)}) async-start(), calls=%async_computation.9 | async-start | bytes 4177920 | tf_op jit(solution)/shard_map/reduce_scatter | solution.py:133
  24.1 22.4 %copy-start.101 = (bf16[2,3,768,192]{2,3,1,0:T(8,128)(2,1)S(1)}, bf16[2,3,768,192]{2,3,1,0:T(8,128)(2,1)}, u32[]{:S(2)}) copy-start(bf16[2,3,768,192]{2,3,1,0:T(8,128)(2,1)} %param.29) | copy-start | bytes 5308420
  63.2 79.0 %all-gather.23.cloned.1.call-start = ((), (), s32[]{:S(2)}) async-start(), calls=%async_computation.20 | async-start | bytes 5898240 | tf_op jit(solution)/shard_map/all_gather | solution.py:191
  66.5 9.1 copy-start.90
  66.5 9.1 copy-start.85
  66.5 9.1 copy-start.86
  66.5 10.0 copy-start.9
  66.5 115.2 %all-gather.25.cloned.1.call-start = ((), (), s32[]{:S(2)}) async-start(), calls=%async_computation.21 | async-start | bytes 5898240 | tf_op jit(solution)/shard_map/all_gather | solution.py:193
  69.9 151.1 %all-gather.17.cloned.1.call-start = ((), (), s32[]{:S(2)}) async-start(), calls=%async_computation.10 | async-start | bytes 4177920 | tf_op jit(solution)/shard_map/all_gather | solution.py:119
  76.5 27.3 %copy-start.80 = (f32[272]{0:T(512)}, f32[272]{0:T(512)S(1)}, u32[]{:S(2)}) copy-start(f32[272]{0:T(512)S(1)} %convolution_reduce_fusion.1) | copy-start | bytes 3268
  76.6 109.7 %copy-start.68 = (f32[272]{0:T(512)}, f32[272]{0:T(512)S(1)}, u32[]{:S(2)}) copy-start(f32[272]{0:T(512)S(1)} %add_divide_fusion) | copy-start | bytes 3268
  103.8 44.5 %copy-start.13 = (f32[1,272,768]{2,1,0:T(8,128)}, f32[1,272,768]{2,1,0:T(8,128)S(1)}, u32[]{:S(2)}) copy-start(f32[1,272,768]{2,1,0:T(8,128)S(1)} %get-tuple-element.417) | copy-start | bytes 2506756
  103.8 44.4 %copy-start.66 = (f32[272]{0:T(512)}, f32[272]{0:T(512)S(1)}, u32[]{:S(2)}) copy-start(f32[272]{0:T(512)S(1)} %broadcast_multiply_fusion.10) | copy-start | bytes 3268
  104.1 44.2 %copy-start.75 = (f32[272]{0:T(512)}, f32[272]{0:T(512)S(1)}, u32[]{:S(2)}) copy-start(f32[272]{0:T(512)S(1)} %add_rsqrt_fusion.2) | copy-start | bytes 3268
  191.2 129.5 %reduce-scatter.11.cloned.1.call-start = ((), (), s32[]{:S(2)}) async-start(), calls=%async_computation.11 | async-start | bytes 8355840 | tf_op jit(solution)/shard_map/reduce_scatter | solution.py:133
  259.5 100.8 %all-gather.27.cloned.1.call-start = ((), (), s32[]{:S(2)}) async-start(), calls=%async_computation.22 | async-start | bytes 5898240 | tf_op jit(solution)/shard_map/all_gather | solution.py:191
  260.3 139.7 %all-gather.29.cloned.1.call-start = ((), (), s32[]{:S(2)}) async-start(), calls=%async_computation.23 | async-start | bytes 5898240 | tf_op jit(solution)/shard_map/all_gather | solution.py:193
  261.0 184.3 %all-gather.19.cloned.1.call-start = ((), (), s32[]{:S(2)}) async-start(), calls=%async_computation.12 | async-start | bytes 4177920 | tf_op jit(solution)/shard_map/all_gather | solution.py:154
  399.9 8.4 copy-start.11
  399.9 8.4 copy-start.99
  412.7 32.6 %copy-start.44 = (bf16[2,192,768]{2,1,0:T(8,128)(2,1)S(1)}, bf16[2,192,768]{2,1,0:T(8,128)(2,1)}, u32[]{:S(2)}) copy-start(bf16[2,192,768]{2,1,0:T(8,128)(2,1)} %param.31) | copy-start | bytes 1769476
  415.5 129.1 %reduce-scatter.13.cloned.1.call-start = ((), (), s32[]{:S(2)}) async-start(), calls=%async_computation.13 | async-start | bytes 4177920 | tf_op jit(solution)/shard_map/reduce_scatter | solution.py:174
  505.2 94.7 %all-gather.21.cloned.1.call-start = ((), (), s32[]{:S(2)}) async-start(), calls=%async_computation.14 | async-start | bytes 2088960 | tf_op jit(solution)/shard_map/all_gather | solution.py:154
  553.0 8.0 copy-start.17
  553.9 7.1 copy-start.52
  553.9 7.1 copy-start.14
  553.9 7.1 copy-start.61
  553.9 7.1 copy-start.67
  553.9 7.1 copy-start.76
  566.9 9.7 copy-start.78
  568.8 72.4 %reduce-scatter.19.cloned.1.call-start = ((), (), s32[]{:S(2)}) async-start(), calls=%async_computation.17 | async-start | bytes 5898240 | tf_op jit(solution)/shard_map/reduce_scatter | solution.py:224
  576.6 114.5 %reduce-scatter.17.cloned.1.call-start = ((), (), s32[]{:S(2)}) async-start(), calls=%async_computation.16 | async-start | bytes 5898240 | tf_op jit(solution)/shard_map/reduce_scatter | solution.py:224
  583.7 157.9 %reduce-scatter.23.cloned.1.call-start = ((), (), s32[]{:S(2)}) async-start(), calls=%async_computation.19 | async-start | bytes 5898240 | tf_op jit(solution)/shard_map/reduce_scatter | solution.py:230
  592.5 199.3 %reduce-scatter.21.cloned.1.call-start = ((), (), s32[]{:S(2)}) async-start(), calls=%async_computation.18 | async-start | bytes 5898240 | tf_op jit(solution)/shard_map/reduce_scatter | solution.py:230
  599.8 8.5 copy-start.1
  599.8 8.5 copy-start.3
  599.8 8.5 copy-start.55
  599.8 8.5 copy-start.57
  599.8 271.3 %reduce-scatter.15.cloned.1.call-start = ((), (), s32[]{:S(2)}) async-start(), calls=%async_computation.15 | async-start | bytes 2088960 | tf_op jit(solution)/shard_map/reduce_scatter | solution.py:174
  622.7 6.8 copy-start.47
  629.5 437.1 %all-reduce.9.cloned.1.call-start = ((), (), s32[]{:S(2)}) async-start(), calls=%async_computation.24 | async-start | bytes 14155776 | tf_op jit(solution)/shard_map/psum | solution.py:355
  800.1 15.6 %copy-start.81 = (f32[272]{0:T(512)S(1)}, f32[272]{0:T(512)}, u32[]{:S(2)}) copy-start(f32[272]{0:T(512)} %copy-done.80) | copy-start | bytes 3268
  800.1 38.8 %copy-start.8 = (bf16[272,768]{1,0:T(8,128)(2,1)S(1)}, bf16[272,768]{1,0:T(8,128)(2,1)}, u32[]{:S(2)}) copy-start(bf16[272,768]{1,0:T(8,128)(2,1)} %copy-done.7) | copy-start | bytes 1253380
  808.2 63.0 %copy-start.59 = (f32[768]{0:T(1024)S(1)}, f32[768]{0:T(1024)}, u32[]{:S(2)}) copy-start(f32[768]{0:T(1024)} %copy-done.58) | copy-start | bytes 9220
  808.2 63.0 %copy-start.63 = (f32[272]{0:T(512)S(1)}, f32[272]{0:T(512)}, u32[]{:S(2)}) copy-start(f32[272]{0:T(512)} %copy-done.62) | copy-start | bytes 3268
  808.2 63.0 %copy-start.65 = (f32[272]{0:T(512)S(1)}, f32[272]{0:T(512)}, u32[]{:S(2)}) copy-start(f32[272]{0:T(512)} %copy-done.64) | copy-start | bytes 3268
  808.2 64.6 %copy-start.16 = (f32[1,272,768]{2,1,0:T(8,128)S(1)}, f32[1,272,768]{2,1,0:T(8,128)}, u32[]{:S(2)}) copy-start(f32[1,272,768]{2,1,0:T(8,128)} %copy-done.13) | copy-start | bytes 2506756
  816.5 19.8 %copy-start.79 = (f32[272]{0:T(512)}, f32[272]{0:T(512)S(1)}, u32[]{:S(2)}) copy-start(f32[272]{0:T(512)S(1)} %subtract_multiply_fusion.2) | copy-start | bytes 3268
  871.1 6.1 copy-start.89
  871.1 6.1 copy-start.73
  871.1 6.1 copy-start.74
  871.1 6.1 copy-start.82
  877.1 193.2 %copy-start.4 = (f32[544,768]{1,0:T(8,128)}, f32[544,768]{1,0:T(8,128)S(1)}, u32[]{:S(2)}) copy-start(f32[544,768]{1,0:T(8,128)S(1)} %scatter_custom_fusion.1) | copy-start | bytes 5013508
  (69 other events, 175.4 us)
Sparse Core Ops, SparseCore 0:
  23.5 22.9 all-gather.14
  63.3 39.1 reduce-scatter.8
  104.7 37.4 all-gather.22
  144.2 37.4 all-gather.24
  191.3 29.6 all-gather.16
  259.6 60.9 reduce-scatter.10
  322.8 37.4 all-gather.26
  362.4 37.4 all-gather.28
  415.6 29.6 all-gather.18
  505.3 39.1 reduce-scatter.12
  568.9 20.2 all-gather.20
  592.3 47.8 reduce-scatter.18
  643.3 47.8 reduce-scatter.16
  693.7 47.8 reduce-scatter.22
  744.0 47.8 reduce-scatter.20
  795.0 28.7 reduce-scatter.14
  829.2 237.3 all-reduce.8
where the time goes:
time: 1090 us; the launch traced here: 1080 us
  waiting for transfers between devices  626 us (57%)
  matrix products  193 us (18%)
  blocking collectives  87.3 us (8%)
  other arithmetic  80 us (7%)
  local copies, waits for them, and re-layouts  77.9 us (7%)
  between operations  16.4 us (2%)
    psum x1, waiting for transfers between devices, body(): lax.psum(qkv_part.astype(jnp.bfloat16), 'dp').astype(jnp.float32)  148 us
    reduce_scatter x2, waiting for transfers between devices, dense_back(): lax.psum_scatter(second_part.astype(jnp.bfloat16), 'tensor', scatter_dime...  97.4 us
    reduce_scatter x2, waiting for transfers between devices, attention_forward(): lax.psum_scatter(jnp.einsum('gle,ed->gld', head_out, out_weights, preferr...  80 us
    all_gather x2, waiting for transfers between devices, dense_forward(): lax.all_gather(first_weights, 'tensor', axis=1, tiled=True)  74.4 us
    all_gather x2, waiting for transfers between devices, dense_forward(): lax.all_gather(second_weights, 'tensor', axis=0, tiled=True)  64.4 us
    reduce_scatter x2, waiting for transfers between devices, dense_back(): lax.psum_scatter(first_part.astype(jnp.bfloat16), 'tensor', scatter_dimen...  49.9 us
    all_gather x2, waiting for transfers between devices, attention_forward(): gathered = lax.all_gather(normed, 'tensor', axis=0, tiled=True)  42.2 us
    psum x1, blocking collectives, body(): lax.psum((router_part, gain_part, shift_part, out_bias_part, second_bias_...  41.6 us
  transfers between devices with their start and end apart: 17, of which 14 were waited for; matrix products, arithmetic and copies ran while one was open for 14% of the time, Pallas kernels for 0%

commit v1 on v0

--- a/solution.py
+++ b/solution.py
@@ -190,7 +190,10 @@
     full_first, full_first_bias, full_second = (
         lax.all_gather(first_weights, "tensor", axis=1, tiled=True),
         lax.all_gather(first_biases, "tensor", axis=0, tiled=True),
-        lax.all_gather(second_weights, "tensor", axis=0, tiled=True),
+        jnp.concatenate(
+            lax.all_to_all(jnp.stack([second_weights] * lax.axis_size("tensor")), "tensor", 0, 0),
+            axis=0,
+        ),
     )
     preact = (
         jnp.einsum("gld,df->glf", normed, full_first, preferred_element_type=jnp.float32)

time: 1090 us -> 1100 us (level)
  waiting for transfers between devices: 626 us -> 446 us
  blocking collectives: 87.3 us -> 254 us
    all_gather x2, blocking collectives: 11 us -> 177 us  [dense_forward(): lax.all_gather(first_biases, 'tensor', axis=0, tiled=True)]
    reduce_scatter x2, waiting for transfers between devices: 80 us -> 0.04 us  [attention_forward(): lax.psum_scatter(jnp.einsum('gle,ed->gld', head_out, out_weights, preferr...]
    all_gather x2 -> x0, waiting for transfers between devices: 64.4 us -> none  [dense_forward(): lax.all_gather(second_weights, 'tensor', axis=0, tiled=True)]
    all_gather x2, waiting for transfers between devices: 74.4 us -> 42.6 us  [dense_forward(): lax.all_gather(first_weights, 'tensor', axis=1, tiled=True)]
  transfers between devices with their start and end apart: 17 -> 17, of which waited for: 14 -> 10; matrix products, arithmetic and copies ran while one was open for 14% -> 15% of each run, Pallas kernels for 0% -> 0%
where the time goes in v1:
time: 1100 us; the launch traced here: 1090 us
  waiting for transfers between devices  446 us (41%)
  blocking collectives  254 us (23%)
  matrix products  193 us (18%)
  local copies, waits for them, and re-layouts  84.1 us (8%)
  other arithmetic  82.1 us (7%)
  between operations  16.5 us (2%)
  starting transfers between devices  11.8 us (1%)
    all_gather x2, blocking collectives, dense_forward(): lax.all_gather(first_biases, 'tensor', axis=0, tiled=True)  177 us
    psum x1, waiting for transfers between devices, body(): lax.psum(qkv_part.astype(jnp.bfloat16), 'dp').astype(jnp.float32)  145 us
    reduce_scatter x2, waiting for transfers between devices, dense_back(): lax.psum_scatter(second_part.astype(jnp.bfloat16), 'tensor', scatter_dime...  97.6 us
    reduce_scatter x2, waiting for transfers between devices, dense_back(): lax.psum_scatter(first_part.astype(jnp.bfloat16), 'tensor', scatter_dimen...  49.3 us
    all_gather x2, waiting for transfers between devices, dense_forward(): lax.all_gather(first_weights, 'tensor', axis=1, tiled=True)  42.6 us
    all_gather x2, waiting for transfers between devices, attention_forward(): gathered = lax.all_gather(normed, 'tensor', axis=0, tiled=True)  42.4 us
    psum x1, blocking collectives, body(): lax.psum((router_part, gain_part, shift_part, out_bias_part, second_bias_...  41.5 us
    reduce_scatter x2, waiting for transfers between devices, attention_back(): lax.psum_scatter(jnp.einsum('glce,cde->gld', proj_grad, qkv_weights, pref...  39.1 us
  transfers between devices with their start and end apart: 17, of which 10 were waited for; matrix products, arithmetic and copies ran while one was open for 15% of the time, Pallas kernels for 0%

profile of v1, /device:TPU:0, one launch (start us, length us, event | category | flops | bytes accessed | tf_op | source)
XLA Modules:
  0.0 1087.4 jit_solution(2093729707928713685)
XLA Ops:
  8.0 13.7 %gather_fusion = bf16[272,768]{1,0:T(8,128)(2,1)S(1)} fusion(bf16[1,544,768]{2,1,0:T(8,128)(2,1)} %param.23, s32[272]{0:T(512)S(1)} %get-tuple-element.320), kind=kCustom, calls=%fused_computation | custom fusion | bytes 837760 | tf_op jit(solution)/shard_map/gather | solution.py:269
  24.1 9.3 gather_fusion.2
  33.6 12.8 %all-gather.11.cloned.1.call-done = bf16[4,272,768]{2,1,0:T(8,128)(2,1)} async-done(((bf16[1,272,768]{2,1,0:T(8,128)(2,1)}), bf16[4,272,768]{2,1,0:T(8,128)(2,1)}) %all-gather.11.cloned.1.call-update) | async-done | bytes 1671184 | tf_op jit(solution)/shard_map/all_gather | solution.py:119
  46.5 2.9 fusion.146
  55.6 5.0 while.52
  63.3 3.3 fusion.255
  67.8 2.5 stack.192
  70.3 5.2 all-to-all-start
  75.6 86.8 %all-gather.1 = bf16[1,3072]{1,0:T(2,128)(2,1)S(1)} all-gather(bf16[1,768]{1,0:T(2,128)(2,1)S(1)} %get-tuple-element.434), channel_id=3, replica_groups=mesh['dp'=8,'tensor'=4] {'tensor'}, dimensions={1}, use_global_device_ids=true | all-gather | bytes 7680 | tf_op jit(solution)/shard_map/all_gather | solution.py:192
  165.2 8.9 all-gather.19.cloned.1.call-done
  174.1 6.1 multiply_convert_fusion.3
  180.2 4.5 fusion.165
  184.8 3.1 scatter_custom_fusion
  189.9 29.5 %all-gather.13.cloned.1.call-done = bf16[4,544,768]{2,1,0:T(8,128)(2,1)} async-done(((bf16[1,544,768]{2,1,0:T(8,128)(2,1)}), bf16[4,544,768]{2,1,0:T(8,128)(2,1)}) %all-gather.13.cloned.1.call-update) | async-done | bytes 3342352 | tf_op jit(solution)/shard_map/all_gather | solution.py:119
  219.5 4.7 fusion.135
  227.9 25.0 %while.53 = (s32[]{:T(128)}, bf16[4,1,544,3,64]{2,4,3,1,0:T(8,128)(2,1)}, f32[4,1,3,544]{3,2,1,0:T(4,128)S(1)}, bf16[4,1,544,3,64]{2,4,3,1,0:T(8,128)(2,1)}, s32...) while((s32[]{:T(128)}, ...), condition=%wide.region_17.18_spmd, body=%wide.region_14.17_spmd.sunk | while | flops 238331296 | bytes 12944741 | solution.py:59
  231.1 3.0 fusion.326
  237.3 3.0 fusion.326
  243.6 3.0 fusion.326
  249.9 3.0 fusion.326
  252.9 5.1 fusion.226
  258.6 3.8 stack.193
  262.4 5.0 all-to-all-start.1
  267.4 90.5 %all-gather.3 = bf16[1,3072]{1,0:T(2,128)(2,1)S(1)} all-gather(bf16[1,768]{1,0:T(2,128)(2,1)S(1)} %get-tuple-element.433), channel_id=5, replica_groups=mesh['dp'=8,'tensor'=4] {'tensor'}, dimensions={1}, use_global_device_ids=true | all-gather | bytes 7680 | tf_op jit(solution)/shard_map/all_gather | solution.py:192
  361.3 33.7 %all-gather.21.cloned.1.call-done = bf16[1,768,3072]{2,1,0:T(8,128)(2,1)} async-done(((bf16[1,768,768]{2,1,0:T(8,128)(2,1)}), bf16[1,768,3072]{2,1,0:T(8,128)(2,1)}) %all-gather.21.cloned.1.call-update) | async-done | bytes 4718608 | tf_op jit(solution)/shard_map/all_gather | solution.py:191
  395.0 8.6 multiply_convert_fusion.2
  403.6 8.4 fusion.257
  412.0 3.6 fusion.148
  416.4 2.7 convert_reduce_fusion.2
  419.6 29.4 %all-gather.15.cloned.1.call-done = bf16[4,544,768]{2,1,0:T(8,128)(2,1)} async-done(((bf16[1,544,768]{2,1,0:T(8,128)(2,1)}), bf16[4,544,768]{2,1,0:T(8,128)(2,1)}) %all-gather.15.cloned.1.call-update) | async-done | bytes 3342352 | tf_op jit(solution)/shard_map/all_gather | solution.py:154
  449.0 4.1 convolution_convert_fusion.4
  456.4 45.8 %while.54 = (s32[]{:T(128)}, bf16[4,1,544,3,64]{2,4,3,1,0:T(8,128)(2,1)}, bf16[4,1,544,3,64]{2,4,3,1,0:T(8,128)(2,1)}, bf16[4,1,544,3,64]{2,4,3,1,0:T(8,128)(2,1...) while((s32[]{:T(128)}, ...), condition=%wide.region_25.26_spmd, body=%wide.region_23.25_spmd.sunk | while | flops 582330752 | bytes 35354008 | solution.py:59
  458.6 2.5 multiply_reduce_fusion.9
  470.0 2.5 multiply_reduce_fusion.9
  481.5 2.5 multiply_reduce_fusion.9
  492.9 2.5 multiply_reduce_fusion.9
  502.2 6.6 bitcast_convert_fusion
  509.1 39.1 %reduce-scatter.13.cloned.1.call-done = bf16[1,544,768]{2,1,0:T(8,128)(2,1)} async-done(((bf16[4,544,768]{2,1,0:T(8,128)(2,1)}), bf16[1,544,768]{2,1,0:T(8,128)(2,1)}) %reduce-scatter.13.cloned.1.call-update) | async-done | bytes 835600 | tf_op jit(solution)/shard_map/reduce_scatter | solution.py:174
  548.2 2.6 fusion.143
  552.9 4.3 gather_fusion.1
  557.3 7.3 fusion.258
  564.6 5.2 fusion.195
  572.4 7.7 convolution_convert_fusion.3
  581.3 6.0 convolution_convert_fusion.1
  588.5 7.6 convolution_convert_fusion.2
  597.2 6.2 convolution_convert_fusion
  604.6 3.2 convolution_convert_fusion.5
  611.9 13.0 %while.55 = (s32[]{:T(128)}, bf16[2,2,272,3,64]{2,4,3,1,0:T(8,128)(2,1)}, bf16[2,2,272,3,64]{2,4,3,1,0:T(8,128)(2,1)}, bf16[2,2,272,3,64]{2,4,3,1,0:T(8,128)(2,1...) while((s32[]{:T(128)}, ...), condition=%wide.region_34.35_spmd, body=%wide.region_32.34_spmd.sunk | while | flops 288762272 | bytes 28893860 | solution.py:59
  629.5 4.3 bitcast_convert_fusion.1
  634.2 3.3 fusion.169
  645.5 49.3 %reduce-scatter.17.cloned.1.call-done = bf16[768,768]{1,0:T(8,128)(2,1)} async-done(((bf16[768,3072]{1,0:T(8,128)(2,1)}), bf16[768,768]{1,0:T(8,128)(2,1)}) %reduce-scatter.17.cloned.1.call-update) | async-done | bytes 1179664 | tf_op jit(solution)/shard_map/reduce_scatter | solution.py:227
  694.8 3.2 pad_maximum_fusion.1
  698.0 47.2 %reduce-scatter.23.cloned.1.call-done = bf16[768,768]{1,0:T(8,128)(2,1)} async-done(((bf16[3072,768]{1,0:T(8,128)(2,1)}), bf16[768,768]{1,0:T(8,128)(2,1)}) %reduce-scatter.23.cloned.1.call-update) | async-done | bytes 1179664 | tf_op jit(solution)/shard_map/reduce_scatter | solution.py:233
  745.2 50.4 %reduce-scatter.21.cloned.1.call-done = bf16[768,768]{1,0:T(8,128)(2,1)} async-done(((bf16[3072,768]{1,0:T(8,128)(2,1)}), bf16[768,768]{1,0:T(8,128)(2,1)}) %reduce-scatter.21.cloned.1.call-update) | async-done | bytes 1179664 | tf_op jit(solution)/shard_map/reduce_scatter | solution.py:233
  795.6 3.2 pad_maximum_fusion.2
  805.1 7.5 fusion.152
  828.2 11.3 %all-reduce.6 = (bf16[3072]{0:T(1024)(128)(2,1)}, bf16[3072]{0:T(1024)(128)(2,1)}) all-reduce(bf16[3072]{0:T(1024)(128)(2,1)} %get-tuple-element.441, bf16[3072]{0:T(1024)(128)(2,1)} %get-tuple-element.443), channel_id=13, replica_groups=mesh['dp'=8,'tensor'=4] {'tensor'}, use_global_device_ids=true, to_apply=%region_66.67.clone | all-reduce | flops 6144 | bytes 24576
  853.2 23.6 %all-reduce.4 = (bf16[2,2,192]{2,1,0:T(2,128)(2,1)S(1)}, bf16[2,768]{1,0:T(2,128)(2,1)S(1)}) all-reduce(bf16[2,2,192]{2,1,0:T(2,128)(2,1)S(1)} %pad_maximum_fusion.15, bf16[2,768]{1,0:T(2,128)(2,1)} %pad_maximum_fusion.14), channel_id=1, replica_groups=mesh['dp'=8,'tensor'=4] {'dp'}, use_global_device_ids=true, to_apply=%region_55.56 | all-reduce | flops 2304 | bytes 9216 | tf_op jit(solution)/shard_map/psum | solution.py:359
  879.6 4.6 scatter_custom_fusion.1
  884.3 41.5 %all-reduce.3 = (f32[768]{0:T(1024)}, f32[2,2,768]{2,1,0:T(2,128)}, f32[2,2,768]{2,1,0:T(2,128)}, f32[2,768]{1,0:T(2,128)}, f32[2,768]{1,0:T(2,128)}) all-reduce(f32[768]{0:T(1024)S(1)} %copy-done.86, f32[2,2,768]{2,1,0:T(2,128)S(1)} %pad_maximum_fusion.10, ...), channel_id=1, replica_groups=mesh['dp'=8,'tensor'=4] {'dp','tensor'}, use_global_device_ids=true, to_apply=%region_39.40 | all-reduce | flops 9984 | bytes 79872 | tf_op jit(solution)/shard_map/psum | solution.py:348
  925.8 144.6 %all-reduce.9.cloned.1.call-done = (bf16[2,3,768,192]{2,3,1,0:T(8,128)(2,1)}, bf16[2,192,768]{2,1,0:T(8,128)(2,1)}, bf16[2,768,768]{2,1,0:T(8,128)(2,1)}, bf16[2,768,768]{2,1,0:T(8,128)(2,1)}) async-done(((bf16[2,3,768,192]{2,3,1,0:T(8,128)(2,1)}, bf16[2,192,768]{2,1,0:T(8,128)(2,1)}, bf16[2,768,768]{2,1,0:T(8,128)(2,1)}, bf16[2,768,768]{2,1,0:T(8,128)(2,1)}), (bf16[2,3,768,192]{2,3,1,0:T(8,128)(2,1)}, ...) | async-done | bytes 7077904 | tf_op jit(solution)/shard_map/psum | solution.py:358
  1070.5 3.7 convert_element_type.444
  1075.3 2.5 convert_element_type.455
  1077.9 2.5 convert_element_type.460
  (495 shorter events, 161.2 us)
Async XLA Ops:
  7.2 15.1 %copy-start.75 = (bf16[2,2,768]{2,1,0:T(2,128)(2,1)S(1)}, bf16[2,2,768]{2,1,0:T(2,128)(2,1)}, u32[]{:S(2)}) copy-start(bf16[2,2,768]{2,1,0:T(2,128)(2,1)} %param.28) | copy-start | bytes 18436
  7.2 15.1 %copy-start.76 = (bf16[2,2,768]{2,1,0:T(2,128)(2,1)S(1)}, bf16[2,2,768]{2,1,0:T(2,128)(2,1)}, u32[]{:S(2)}) copy-start(bf16[2,2,768]{2,1,0:T(2,128)(2,1)} %param.27) | copy-start | bytes 18436
  7.2 39.3 %all-gather.11.cloned.1.call-start = ((), (), s32[]{:S(2)}) async-start(), calls=%async_computation.10 | async-start | bytes 2088960 | tf_op jit(solution)/shard_map/all_gather | solution.py:119
  8.0 15.4 %copy-start.5 = (s32[272]{0:T(512)}, s32[272]{0:T(512)S(1)}, u32[]{:S(2)}) copy-start(s32[272]{0:T(512)S(1)} %get-tuple-element.320) | copy-start | bytes 3268
  8.0 176.8 %copy-start.101 = (s32[272]{0:T(512)}, s32[272]{0:T(512)S(1)}, u32[]{:S(2)}) copy-start(s32[272]{0:T(512)S(1)} %get-tuple-element.321) | copy-start | bytes 3268
  8.0 15.5 %copy-start.96 = (bf16[2,2,192]{2,1,0:T(2,128)(2,1)S(1)}, bf16[2,2,192]{2,1,0:T(2,128)(2,1)}, u32[]{:S(2)}) copy-start(bf16[2,2,192]{2,1,0:T(2,128)(2,1)} %param.30) | copy-start | bytes 4612
  8.0 15.6 %copy-start.102 = (s32[4,6]{1,0:T(4,128)S(1)}, s32[4,6]{1,0:T(4,128)}, u32[]{:S(2)}) copy-start(s32[4,6]{1,0:T(4,128)} %param.24) | copy-start | bytes 292
  8.0 15.9 %copy-start.74 = (s32[4,272]{1,0:T(4,128)S(1)}, s32[4,272]{1,0:T(4,128)}, u32[]{:S(2)}) copy-start(s32[4,272]{1,0:T(4,128)} %param.25) | copy-start | bytes 13060
  21.8 141.8 %copy-start.7 = (bf16[272,768]{1,0:T(8,128)(2,1)}, bf16[272,768]{1,0:T(8,128)(2,1)S(1)}, u32[]{:S(2)}) copy-start(bf16[272,768]{1,0:T(8,128)(2,1)S(1)} %gather_fusion) | copy-start | bytes 1253380
  22.3 151.8 %copy-start.64 = (f32[768]{0:T(1024)}, f32[768]{0:T(1024)S(1)}, u32[]{:S(2)}) copy-start(f32[768]{0:T(1024)S(1)} %get-tuple-element.447) | copy-start | bytes 9220
  22.4 151.8 %copy-start.97 = (f32[768]{0:T(1024)}, f32[768]{0:T(1024)S(1)}, u32[]{:S(2)}) copy-start(f32[768]{0:T(1024)S(1)} %get-tuple-element.313) | copy-start | bytes 9220
  22.4 166.1 %copy-start.60 = (f32[768]{0:T(1024)}, f32[768]{0:T(1024)S(1)}, u32[]{:S(2)}) copy-start(f32[768]{0:T(1024)S(1)} %get-tuple-element.445) | copy-start | bytes 9220
  23.4 140.1 %reduce-scatter.9.cloned.1.call-start = ((), (), s32[]{:S(2)}) async-start(), calls=%async_computation.11 | async-start | bytes 4177920 | tf_op jit(solution)/shard_map/reduce_scatter | solution.py:133
  24.1 22.4 %copy-start.105 = (bf16[2,3,768,192]{2,3,1,0:T(8,128)(2,1)S(1)}, bf16[2,3,768,192]{2,3,1,0:T(8,128)(2,1)}, u32[]{:S(2)}) copy-start(bf16[2,3,768,192]{2,3,1,0:T(8,128)(2,1)} %param.29) | copy-start | bytes 5308420
  63.2 110.9 %all-gather.19.cloned.1.call-start = ((), (), s32[]{:S(2)}) async-start(), calls=%async_computation.22 | async-start | bytes 5898240 | tf_op jit(solution)/shard_map/all_gather | solution.py:191
  70.3 92.1 %copy-start.94 = (bf16[768]{0:T(1024)(128)(2,1)S(1)}, bf16[768]{0:T(1024)(128)(2,1)}, u32[]{:S(2)}) copy-start(bf16[768]{0:T(1024)(128)(2,1)} %param.26) | copy-start | bytes 4612
  70.3 92.1 %copy-start.89 = (bf16[2,768]{1,0:T(2,128)(2,1)S(1)}, bf16[2,768]{1,0:T(2,128)(2,1)}, u32[]{:S(2)}) copy-start(bf16[2,768]{1,0:T(2,128)(2,1)} %param.32) | copy-start | bytes 9220
  70.3 92.1 %copy-start.90 = (bf16[2,768]{1,0:T(2,128)(2,1)S(1)}, bf16[2,768]{1,0:T(2,128)(2,1)}, u32[]{:S(2)}) copy-start(bf16[2,768]{1,0:T(2,128)(2,1)} %param.36) | copy-start | bytes 9220
  70.3 93.0 %copy-start.9 = (bf16[1,544,768]{2,1,0:T(8,128)(2,1)S(1)}, bf16[1,544,768]{2,1,0:T(8,128)(2,1)}, u32[]{:S(2)}) copy-start(bf16[1,544,768]{2,1,0:T(8,128)(2,1)} %param.23) | copy-start | bytes 2506756
  70.3 109.9 %all-to-all-start = ((bf16[4,768,768]{2,1,0:T(8,128)(2,1)}), bf16[4,768,768]{2,1,0:T(8,128)(2,1)}, u32[]{:S(2)}, u32[]{:S(2)}) async-start(bf16[4,768,768]{2,1,0:T(8,128)(2,1)} %stack.192), calls=%async_computation.1 | async-start | bytes 9437184 | tf_op jit(solution)/shard_map/all_to_all | solution.py:194
  75.5 144.0 %all-gather.13.cloned.1.call-start = ((), (), s32[]{:S(2)}) async-start(), calls=%async_computation.12 | async-start | bytes 4177920 | tf_op jit(solution)/shard_map/all_gather | solution.py:119
  163.4 21.4 %copy-start.72 = (f32[272]{0:T(512)}, f32[272]{0:T(512)S(1)}, u32[]{:S(2)}) copy-start(f32[272]{0:T(512)S(1)} %add_divide_fusion) | copy-start | bytes 3268
  164.9 15.3 %copy-start.14 = (f32[1,272,768]{2,1,0:T(8,128)}, f32[1,272,768]{2,1,0:T(8,128)S(1)}, u32[]{:S(2)}) copy-start(f32[1,272,768]{2,1,0:T(8,128)S(1)} %get-tuple-element.415) | copy-start | bytes 2506756
  164.9 15.3 %copy-start.70 = (f32[272]{0:T(512)}, f32[272]{0:T(512)S(1)}, u32[]{:S(2)}) copy-start(f32[272]{0:T(512)S(1)} %broadcast_multiply_fusion.10) | copy-start | bytes 3268
  165.2 15.0 %copy-start.79 = (f32[272]{0:T(512)}, f32[272]{0:T(512)S(1)}, u32[]{:S(2)}) copy-start(f32[272]{0:T(512)S(1)} %add_rsqrt_fusion.2) | copy-start | bytes 3268
  188.4 35.7 %copy-start.62 = (f32[544]{0:T(1024)}, f32[544]{0:T(1024)S(1)}, u32[]{:S(2)}) copy-start(f32[544]{0:T(1024)S(1)} %add_rsqrt_fusion.1) | copy-start | bytes 6532
  189.7 168.3 %reduce-scatter.11.cloned.1.call-start = ((), (), s32[]{:S(2)}) async-start(), calls=%async_computation.13 | async-start | bytes 8355840 | tf_op jit(solution)/shard_map/reduce_scatter | solution.py:133
  258.0 136.9 %all-gather.21.cloned.1.call-start = ((), (), s32[]{:S(2)}) async-start(), calls=%async_computation.23 | async-start | bytes 5898240 | tf_op jit(solution)/shard_map/all_gather | solution.py:191
  262.4 141.2 %all-to-all-start.1 = ((bf16[4,768,768]{2,1,0:T(8,128)(2,1)}), bf16[4,768,768]{2,1,0:T(8,128)(2,1)}, u32[]{:S(2)}, u32[]{:S(2)}) async-start(bf16[4,768,768]{2,1,0:T(8,128)(2,1)} %stack.193), calls=%async_computation.3 | async-start | bytes 9437184 | tf_op jit(solution)/shard_map/all_to_all | solution.py:194
  267.4 181.6 %all-gather.15.cloned.1.call-start = ((), (), s32[]{:S(2)}) async-start(), calls=%async_computation.14 | async-start | bytes 4177920 | tf_op jit(solution)/shard_map/all_gather | solution.py:154
  403.6 8.5 copy-start.11
  403.6 8.5 copy-start.103
  416.4 32.6 %copy-start.47 = (bf16[2,192,768]{2,1,0:T(8,128)(2,1)S(1)}, bf16[2,192,768]{2,1,0:T(8,128)(2,1)}, u32[]{:S(2)}) copy-start(bf16[2,192,768]{2,1,0:T(8,128)(2,1)} %param.31) | copy-start | bytes 1769476
  419.2 129.0 %reduce-scatter.13.cloned.1.call-start = ((), (), s32[]{:S(2)}) async-start(), calls=%async_computation.15 | async-start | bytes 4177920 | tf_op jit(solution)/shard_map/reduce_scatter | solution.py:174
  508.9 39.3 %copy-start.57 = (f32[544]{0:T(1024)S(1)}, f32[544]{0:T(1024)}, u32[]{:S(2)}) copy-start(f32[544]{0:T(1024)} %copy-done.56) | copy-start | bytes 6532
  508.9 39.3 %copy-start.61 = (f32[768]{0:T(1024)S(1)}, f32[768]{0:T(1024)}, u32[]{:S(2)}) copy-start(f32[768]{0:T(1024)} %copy-done.60) | copy-start | bytes 9220
  508.9 39.3 %copy-start.63 = (f32[544]{0:T(1024)S(1)}, f32[544]{0:T(1024)}, u32[]{:S(2)}) copy-start(f32[544]{0:T(1024)} %copy-done.62) | copy-start | bytes 6532
  508.9 94.7 %all-gather.17.cloned.1.call-start = ((), (), s32[]{:S(2)}) async-start(), calls=%async_computation.16 | async-start | bytes 2088960 | tf_op jit(solution)/shard_map/all_gather | solution.py:154
  557.2 7.3 copy-start.18
  557.3 7.3 copy-start.15
  557.3 7.3 copy-start.65
  557.3 7.3 copy-start.71
  557.3 7.3 copy-start.80
  570.5 9.6 copy-start.82
  572.4 73.1 %reduce-scatter.19.cloned.1.call-start = ((), (), s32[]{:S(2)}) async-start(), calls=%async_computation.19 | async-start | bytes 5898240 | tf_op jit(solution)/shard_map/reduce_scatter | solution.py:227
  580.2 114.6 %reduce-scatter.17.cloned.1.call-start = ((), (), s32[]{:S(2)}) async-start(), calls=%async_computation.18 | async-start | bytes 5898240 | tf_op jit(solution)/shard_map/reduce_scatter | solution.py:227
  587.3 157.9 %reduce-scatter.23.cloned.1.call-start = ((), (), s32[]{:S(2)}) async-start(), calls=%async_computation.21 | async-start | bytes 5898240 | tf_op jit(solution)/shard_map/reduce_scatter | solution.py:233
  596.1 199.5 %reduce-scatter.21.cloned.1.call-start = ((), (), s32[]{:S(2)}) async-start(), calls=%async_computation.20 | async-start | bytes 5898240 | tf_op jit(solution)/shard_map/reduce_scatter | solution.py:233
  603.5 8.4 copy-start.1
  603.5 8.4 copy-start.3
  603.5 8.4 copy-start.53
  603.5 8.4 copy-start.55
  603.5 274.4 %reduce-scatter.15.cloned.1.call-start = ((), (), s32[]{:S(2)}) async-start(), calls=%async_computation.17 | async-start | bytes 2088960 | tf_op jit(solution)/shard_map/reduce_scatter | solution.py:174
  633.8 436.6 %all-reduce.9.cloned.1.call-start = ((), (), s32[]{:S(2)}) async-start(), calls=%async_computation.24 | async-start | bytes 14155776 | tf_op jit(solution)/shard_map/psum | solution.py:358
  805.1 15.0 %copy-start.85 = (f32[272]{0:T(512)S(1)}, f32[272]{0:T(512)}, u32[]{:S(2)}) copy-start(f32[272]{0:T(512)} %copy-done.84) | copy-start | bytes 3268
  812.6 33.0 %copy-start.8 = (bf16[272,768]{1,0:T(8,128)(2,1)S(1)}, bf16[272,768]{1,0:T(8,128)(2,1)}, u32[]{:S(2)}) copy-start(bf16[272,768]{1,0:T(8,128)(2,1)} %copy-done.7) | copy-start | bytes 1253380
  812.6 37.7 %copy-start.26 = (bf16[2,2,272,3,64]{2,4,3,1,0:T(8,128)(2,1)S(1)}, bf16[2,2,272,3,64]{2,4,3,1,0:T(8,128)(2,1)}, u32[]{:S(2)}) copy-start(bf16[2,2,272,3,64]{2,4,3,1,0:T(8,128)(2,1)} %get-tuple-element.204) | copy-start | bytes 1253380
  812.6 65.4 %copy-start.59 = (f32[768]{0:T(1024)S(1)}, f32[768]{0:T(1024)}, u32[]{:S(2)}) copy-start(f32[768]{0:T(1024)} %copy-done.58) | copy-start | bytes 9220
  812.6 65.4 %copy-start.67 = (f32[272]{0:T(512)S(1)}, f32[272]{0:T(512)}, u32[]{:S(2)}) copy-start(f32[272]{0:T(512)} %copy-done.66) | copy-start | bytes 3268
  812.6 65.4 %copy-start.69 = (f32[272]{0:T(512)S(1)}, f32[272]{0:T(512)}, u32[]{:S(2)}) copy-start(f32[272]{0:T(512)} %copy-done.68) | copy-start | bytes 3268
  814.7 64.9 %copy-start.17 = (f32[1,272,768]{2,1,0:T(8,128)S(1)}, f32[1,272,768]{2,1,0:T(8,128)}, u32[]{:S(2)}) copy-start(f32[1,272,768]{2,1,0:T(8,128)} %copy-done.14) | copy-start | bytes 2506756
  820.7 22.2 %copy-start.83 = (f32[272]{0:T(512)}, f32[272]{0:T(512)S(1)}, u32[]{:S(2)}) copy-start(f32[272]{0:T(512)S(1)} %subtract_multiply_fusion.2) | copy-start | bytes 3268
  877.9 6.4 copy-start.86
  884.2 190.0 %copy-start.4 = (f32[544,768]{1,0:T(8,128)}, f32[544,768]{1,0:T(8,128)S(1)}, u32[]{:S(2)}) copy-start(f32[544,768]{1,0:T(8,128)S(1)} %scatter_custom_fusion.1) | copy-start | bytes 5013508
  (73 other events, 208.4 us)
Sparse Core Ops, SparseCore 0:
  23.5 22.9 all-gather.10
  63.3 57.1 reduce-scatter.8
  122.7 51.3 all-gather.18
  189.8 29.6 all-gather.12
  258.2 97.2 reduce-scatter.10
  357.5 37.4 all-gather.20
  419.3 29.6 all-gather.14
  509.0 39.1 reduce-scatter.12
  572.5 20.2 all-gather.16
  595.9 47.8 reduce-scatter.18
  646.9 47.8 reduce-scatter.16
  697.3 47.8 reduce-scatter.22
  747.8 47.8 reduce-scatter.20
  798.8 28.7 reduce-scatter.14
  833.0 237.4 all-reduce.8
